TPU v7x, 1024 devices: a whole 8x8x8 slice. The times are simulated.
1024 devices in a mesh: energy: 32 (over z, y_lo), rows: 32 (over y_hi, x, core).
Axes of the slice: x: 8, y: 8 (y_hi: 2, y_lo: 4; y = y_hi * 4 + y_lo), z: 8, core: 2. Of those that a mesh axis runs over, the one named last changes fastest.
Arguments:
- green_window: bfloat16 [2, 2, 64, 32, 9216], P(None, None, 'energy', 'rows'), may hold values from -6 to 6
- screened: bfloat16 [2, 2, 64, 32, 9216], P(None, None, None, 'rows', 'energy'), may hold values from -6 to 6
- retarded: bfloat16 [2, 64, 32, 3, 96, 192], P(None, 'energy', 'rows'), may hold values from -0.375 to 0.375
- energy_order: int32 [64], replicated, may hold values from 0 to 63, each once
- window_start: int32 [32], P('rows'), may hold values from 0 to 96
Outputs:
- density: float32 [2, 2, 64, 32, 192], P(None, None, 'energy', 'rows')
Inputs may be any that keep to these rules, and one draw needn't show every extreme that they name: A permutation of the energy indices: slot s holds energy energy_order[s]. Block row i's window covers its orbitals window_start[i] to window_start[i] + 95.
All inputs are finite; a program needn't handle non-finite values.
Results may differ from a plain program's by a relative error of at most 0.0029.
Values may be sent and summed in bfloat16 or wider, within the bound.
A program may use at most 32 MiB of HBM per device.

v0:
```python
import math

import jax
import jax.numpy as jnp
from jax import lax
from jax.sharding import PartitionSpec as P


def with_halo(cells, sides, width):
    for axis, dim in sides:
        count = lax.axis_size(axis)
        ends = count - 1
        head = lax.slice_in_dim(cells, 0, width, axis=dim)
        tail = lax.slice_in_dim(cells, cells.shape[dim] - width, cells.shape[dim], axis=dim)
        cells = jnp.concatenate(
            [
                lax.ppermute(tail, axis, [(i, (i + 1) % count) for i in range(ends)]),
                cells,
                lax.ppermute(head, axis, [((i + 1) % count, i) for i in range(ends)]),
            ],
            axis=dim,
        )
    return cells


def phase_table(count_rows, count_cols, modulus, direction):
    left = lax.broadcasted_iota(jnp.int32, (count_rows, count_cols), 0)
    right = lax.broadcasted_iota(jnp.int32, (count_rows, count_cols), 1)
    turns = left * right % modulus
    angle = direction * 2.0 * math.pi / modulus * turns.astype(jnp.float32)
    return (jnp.cos(angle), jnp.sin(angle))


def complex_einsum(form, left_re, left_im, right_re, right_im):
    highest = lax.Precision.HIGHEST
    real_part = jnp.einsum(form, left_re, right_re, precision=highest) - jnp.einsum(
        form, left_im, right_im, precision=highest
    )
    imag_part = jnp.einsum(form, left_re, right_im, precision=highest) + jnp.einsum(
        form, left_im, right_re, precision=highest
    )
    return (real_part, imag_part)


def transform(data_re, data_im, inner_count, direction):
    total = data_re.shape[0]
    columns = data_re.shape[1]
    outer_count = total // inner_count
    shaped_re = data_re.reshape(inner_count, outer_count, columns)
    shaped_im = data_im.reshape(inner_count, outer_count, columns)
    first_re, first_im = phase_table(inner_count, inner_count, inner_count, direction)
    section_re, section_im = complex_einsum("kb,bac->kac", first_re, first_im, shaped_re, shaped_im)
    twist_re, twist_im = phase_table(inner_count, outer_count, total, direction)
    turned_re = section_re * twist_re[:, :, None] - section_im * twist_im[:, :, None]
    turned_im = section_re * twist_im[:, :, None] + section_im * twist_re[:, :, None]
    second_re, second_im = phase_table(outer_count, outer_count, outer_count, direction)
    final_re, final_im = complex_einsum("kac,am->mkc", turned_re, turned_im, second_re, second_im)
    return (final_re.reshape(total, columns), final_im.reshape(total, columns))


def window_product(part, right):
    return jnp.einsum("gepq,epa->geqa", part, right, preferred_element_type=jnp.float32)


def shards(green_window, screened, retarded, energy_order, window_start):
    per_device = green_window.shape[2]
    slab = retarded.shape[4]
    width = retarded.shape[5]
    local = green_window[:, :, :, 0, :]
    spread = lax.all_to_all(local, "energy", split_axis=3, concat_axis=2, tiled=True)
    total = spread.shape[2]
    columns = spread.shape[3]
    inverse = jnp.argsort(energy_order)
    ordered = jnp.take(spread, inverse, axis=2)
    green_cols = (
        jnp.transpose(ordered, (1, 2, 0, 3)).reshape(2, total, 2 * columns).astype(jnp.float32)
    )
    screen_local = screened[:, :, :, 0, :]
    screen_cols = (
        jnp.transpose(screen_local, (1, 2, 0, 3)).reshape(2, total, 2 * columns).astype(jnp.float32)
    )
    times_re, times_im = transform(green_cols[0], green_cols[1], per_device, -1.0)
    mixed_re = times_re * screen_cols[0] - times_im * screen_cols[1]
    mixed_im = times_re * screen_cols[1] + times_im * screen_cols[0]
    back_re, back_im = transform(mixed_re, mixed_im, per_device, 1.0)
    scale = 1.0 / total
    sigma_cols = jnp.stack([-back_im * scale, back_re * scale]).astype(jnp.bfloat16)
    sigma_slots = jnp.take(sigma_cols, energy_order, axis=1)
    sigma = jnp.transpose(sigma_slots.reshape(2, total, 2, columns), (2, 0, 1, 3))
    bordered_entries = with_halo(sigma[:, :, :, None, :], (("rows", 3),), 1)
    bordered = lax.all_to_all(bordered_entries, "energy", split_axis=2, concat_axis=4, tiled=True)
    sigma_all = bordered.reshape(2, 2, per_device, 3, slab, slab)
    dens_re = jnp.zeros((2, per_device, width), jnp.float32)
    dens_im = jnp.zeros((2, per_device, width), jnp.float32)
    for neighbour in range(3):
        part_re = sigma_all[:, 0, :, neighbour]
        part_im = sigma_all[:, 1, :, neighbour]
        right_re = retarded[0, :, 0, neighbour]
        right_im = retarded[1, :, 0, neighbour]
        inner_re = window_product(part_re, right_re) - window_product(part_im, right_im)
        inner_im = window_product(part_re, right_im) + window_product(part_im, right_re)
        wide_re = right_re.astype(jnp.float32)[None]
        wide_im = right_im.astype(jnp.float32)[None]
        dens_re = dens_re + jnp.sum(inner_re * wide_re + inner_im * wide_im, axis=2)
        dens_im = dens_im + jnp.sum(inner_im * wide_re - inner_re * wide_im, axis=2)
    own = sigma_all[:, :, :, 1].astype(jnp.float32)
    diagonal_part = jnp.diagonal(own, axis1=3, axis2=4)
    start = window_start[0]
    column_ids = lax.broadcasted_iota(jnp.int32, (slab, width), 1)
    window_ids = lax.broadcasted_iota(jnp.int32, (slab, width), 0)
    place = (column_ids == window_ids + start).astype(jnp.float32)
    direct = jnp.einsum("gcep,pa->gcea", diagonal_part, place, precision=lax.Precision.HIGHEST)
    density = jnp.stack([dens_re, dens_im], axis=1) + direct
    return density[:, :, :, None, :]


def solution(mesh):
    in_specs = (
        P(None, None, "energy", "rows", None),
        P(None, None, None, "rows", "energy"),
        P(None, "energy", "rows", None, None, None),
        P(),
        P("rows"),
    )
    out_specs = P(None, None, "energy", "rows", None)
    return jax.shard_map(shards, mesh=mesh, in_specs=in_specs, out_specs=out_specs, check_vma=False)
```

profile of v0, /device:TPU:15, one launch (start us, length us, event | category | flops | bytes accessed | tf_op | source)
XLA Modules:
  0.0 202.4 jit_solution(11717727448099971937)
XLA Ops:
  0.0 17.9 %copy.103 = bf16[2,2,2,1,9216]{2,1,0,4,3:T(2,128)(2,1)} copy(bf16[2,2,2,1,9216]{4,2,3,1,0:T(2,128)(2,1)} %param.5) | data formatting | bytes 294912 | tf_op args[0]
  17.9 8.8 %bitcast_bitcast_fusion = bf16[9216,2,2,2]{3,2,1,0:T(2,128)(2,1)} fusion(bf16[2,2,2,1,9216]{2,1,0,4,3:T(2,128)(2,1)} %copy.103), kind=kLoop, calls=%fused_computation.258 | loop fusion | bytes 294912
  26.8 15.2 %reshape.229 = bf16[32,2,1152]{2,1,0:T(2,128)(2,1)} reshape(bf16[9216,2,2,2]{3,2,1,0:T(2,128)(2,1)} %bitcast_bitcast_fusion) | data formatting | bytes 294912
  41.9 20.2 %all-to-all-start = ((bf16[32,2,1152]{2,1,0:T(2,128)(2,1)}), bf16[32,2,1152]{2,1,0:T(2,128)(2,1)S(1)}, u32[]{:S(2)}, u32[]{:S(2)}) async-start(bf16[32,2,1152]{2,1,0:T(2,128)(2,1)} %reshape.229), calls=%async_computation | async-start | bytes 294912 | tf_op jit(solution)/shard_map/all_to_all | solution.py:70
  62.1 2.0 %sort.17 = (s32[64]{0:T(128)}, s32[64]{0:T(128)S(1)}) sort(s32[64]{0:T(128)S(1)} %copy-done.4, s32[64]{0:T(128)S(1)} %iota.170), dimensions={0}, to_apply=%region_0.0 | sort | flops 384 | bytes 1024 | tf_op jit(solution)/shard_map/jit(argsort)/sort | solution.py:73
  64.6 0.2 squeeze.55
  65.0 0.2 squeeze.56
  65.2 7.0 %all-to-all-done = bf16[32,2,1152]{2,1,0:T(2,128)(2,1)S(1)} async-done(((bf16[32,2,1152]{2,1,0:T(2,128)(2,1)}), bf16[32,2,1152]{2,1,0:T(2,128)(2,1)S(1)}, u32[]{:S(2)}, u32[]{:S(2)}) %all-to-all-start) | async-done | bytes 147488 | tf_op jit(solution)/shard_map/all_to_all | solution.py:70
  72.1 21.4 %reshape.230 = bf16[9216,2,2,2]{3,2,1,0:T(2,128)(2,1)} reshape(bf16[32,2,1152]{2,1,0:T(2,128)(2,1)S(1)} %all-to-all-done) | data formatting | bytes 294912
  93.5 20.9 %copy.104 = bf16[2,2,2,32,288]{4,1,2,3,0:T(2,128)(2,1)S(1)} copy(bf16[2,2,2,32,288]{2,1,0,4,3:T(2,128)(2,1)} %bitcast.211) | data formatting | bytes 294912 | tf_op jit(solution)/shard_map/all_to_all | solution.py:70
  114.4 1.0 gather_fusion
  115.4 0.3 fusion.7
  115.7 1.2 slice_reduce_fusion.1
  117.0 0.5 fusion.76
  117.6 0.5 fusion.72
  118.1 0.5 convolution_subtract_fusion.6
  118.6 0.6 multiply_add_fusion.2
  119.2 0.4 fusion.18
  119.5 0.4 fusion.16
  119.9 0.4 convolution_subtract_fusion.4
  120.6 0.4 convolution_add_fusion.4
  121.2 0.7 fusion.24
  122.0 0.8 fusion.20
  122.8 0.8 convolution_subtract_fusion.5
  123.5 0.9 multiply_add_fusion
  124.4 0.4 fusion.12
  124.8 0.4 fusion.10
  125.2 0.4 fusion.4
  125.7 0.4 fusion.3
  126.2 0.4 pad_maximum_fusion.1
  126.6 0.9 gather_fusion.1
  127.5 0.3 gather.16
  127.9 0.3 fusion.6
  128.1 6.9 %collective-permute-start = (bf16[2,2,64,1,288]{4,1,3,0,2:T(2,128)(2,1)S(1)}, bf16[2,2,64,1,288]{4,1,3,0,2:T(2,128)(2,1)S(1)}, u32[]{:S(2)}, u32[]{:S(2)}) collective-permute-start(bf16[2,2,64,1,288]{4,1,3,0,2:T(2,128)(2,1)S(1)} %fusion.6), channel_id=1, source_target_pairs={{0,1},{1,2},{2,3},{3,4},{4,5},{5,6},{6,7},{7,8},{8,9},{9,10},{10,1... | collective-permute-start | bytes 442376 | tf_op jit(solution)/shard_map/ppermute | solution.py:17
  135.1 2.1 %collective-permute-start.1 = (bf16[2,2,64,1,288]{4,1,3,0,2:T(2,128)(2,1)S(1)}, bf16[2,2,64,1,288]{4,1,3,0,2:T(2,128)(2,1)S(1)}, u32[]{:S(2)}, u32[]{:S(2)}) collective-permute-start(bf16[2,2,64,1,288]{4,1,3,0,2:T(2,128)(2,1)S(1)} %fusion.6), channel_id=1, source_target_pairs={{1,0},{2,1},{3,2},{4,3},{5,4},{6,5},{7,6},{8,7},{9,8},{10,9},{11,1... | collective-permute-start | bytes 442376 | tf_op jit(solution)/shard_map/ppermute | solution.py:19
  137.2 0.4 collective-permute-done
  137.7 11.1 %collective-permute-done.1 = bf16[2,2,64,1,288]{4,1,3,0,2:T(2,128)(2,1)S(1)} collective-permute-done((bf16[2,2,64,1,288]{4,1,3,0,2:T(2,128)(2,1)S(1)}, bf16[2,2,64,1,288]{4,1,3,0,2:T(2,128)(2,1)S(1)}, u32[]{:S(2)}, u32[]{:S(2)}) %collective-permute-start.1) | collective-permute-done | bytes 147488 | tf_op jit(solution)/shard_map/ppermute | solution.py:19
  148.8 1.7 pad_maximum_fusion
  150.5 3.9 %all-to-all-start.1 = ((bf16[2,2,64,3,288]{4,1,3,0,2:T(2,128)(2,1)}), bf16[2,2,64,3,288]{4,1,3,0,2:T(2,128)(2,1)S(1)}, u32[]{:S(2)}, u32[]{:S(2)}) async-start(bf16[2,2,64,3,288]{4,1,3,0,2:T(2,128)(2,1)} %pad_maximum_fusion), calls=%async_computation.1 | async-start | bytes 1179648 | tf_op jit(solution)/shard_map/all_to_all | solution.py:91
  155.1 1.1 bitcast_convert_fusion.5
  156.2 11.6 %all-to-all-done.1 = bf16[2,2,64,3,288]{4,1,3,0,2:T(2,128)(2,1)S(1)} async-done(((bf16[2,2,64,3,288]{4,1,3,0,2:T(2,128)(2,1)}), bf16[2,2,64,3,288]{4,1,3,0,2:T(2,128)(2,1)S(1)}, u32[]{:S(2)}, u32[]{:S(2)}) %all-to-all-start.1) | async-done | bytes 442400 | tf_op jit(solution)/shard_map/all_to_all | solution.py:91
  167.9 0.9 reshape.186
  168.8 0.7 fusion.196
  169.6 0.2 fusion.42
  169.8 0.2 fusion.38
  170.1 0.2 fusion.36
  170.3 0.2 fusion.32
  170.6 0.6 copy-done.1
  171.2 0.2 fusion.30
  171.4 1.1 fusion.26
  172.5 0.7 slice.90
  173.2 1.0 copy.163
  174.2 1.0 copy.167
  175.3 1.0 copy.171
  176.3 14.9 %copy.173 = bf16[2,2,2,1,96,96]{2,1,5,4,0,3:T(2,128)(2,1)} copy(bf16[2,2,2,1,96,96]{5,4,3,2,1,0:T(8,128)(2,1)} %slice.90) | data formatting | bytes 294912
  191.2 0.9 convolution_subtract_fusion.2
  192.1 0.2 convolution_subtract_fusion.1
  192.3 0.2 convolution_subtract_fusion
  192.5 4.9 %gather_fusion.2 = bf16[96,2,2,2]{3,2,1,0:T(2,128)(2,1)S(1)} fusion(bf16[2,2,2,96,96]{2,1,4,3,0:T(2,128)(2,1)} %bitcast.212, s32[96]{0:T(128)S(1)} %or_bitcast_fusion), kind=kCustom, calls=%fused_computation.2 | custom fusion | bytes 3840 | tf_op jit(solution)/shard_map/jit(diagonal)/gather | solution.py:107
  197.5 1.5 add_reduce_fusion.2
  198.9 1.3 add_reduce_fusion.1
  200.3 1.3 add_reduce_fusion
  201.6 0.2 fusion.5
  201.8 0.6 copy.152
  (41 shorter events, 2.1 us)
Async XLA Ops:
  26.8 35.4 %copy-start.4 = (s32[64]{0:T(128)S(1)}, s32[64]{0:T(128)}, u32[]{:S(2)}) copy-start(s32[64]{0:T(128)} %param.8) | copy-start | bytes 772
  26.8 37.6 %copy-start.3 = (bf16[2,2,64,1,288]{4,2,3,1,0:T(8,128)(2,1)S(1)}, bf16[2,2,64,1,288]{4,2,3,1,0:T(8,128)(2,1)}, u32[]{:S(2)}) copy-start(bf16[2,2,64,1,288]{4,2,3,1,0:T(8,128)(2,1)} %param.6) | copy-start | bytes 442372
  41.9 30.2 %all-to-all-start = ((bf16[32,2,1152]{2,1,0:T(2,128)(2,1)}), bf16[32,2,1152]{2,1,0:T(2,128)(2,1)S(1)}, u32[]{:S(2)}, u32[]{:S(2)}) async-start(bf16[32,2,1152]{2,1,0:T(2,128)(2,1)} %reshape.229), calls=%async_computation | async-start | bytes 294912 | tf_op jit(solution)/shard_map/all_to_all | solution.py:70
  114.4 40.7 %copy-start = (bf16[2,2,1,3,96,192]{5,4,3,2,1,0:T(8,128)(2,1)S(1)}, bf16[2,2,1,3,96,192]{5,4,3,2,1,0:T(8,128)(2,1)}, u32[]{:S(2)}) copy-start(bf16[2,2,1,3,96,192]{5,4,3,2,1,0:T(8,128)(2,1)} %param.7) | copy-start | bytes 1327108
  128.1 9.5 %collective-permute-start = (bf16[2,2,64,1,288]{4,1,3,0,2:T(2,128)(2,1)S(1)}, bf16[2,2,64,1,288]{4,1,3,0,2:T(2,128)(2,1)S(1)}, u32[]{:S(2)}, u32[]{:S(2)}) collective-permute-start(bf16[2,2,64,1,288]{4,1,3,0,2:T(2,128)(2,1)S(1)} %fusion.6), channel_id=1, source_target_pairs={{0,1},{1,2},{2,3},{3,4},{4,5},{5,6},{6,7},{7,8},{8,9},{9,10},{10,1... | collective-permute-start | bytes 442376 | tf_op jit(solution)/shard_map/ppermute | solution.py:17
  135.1 13.7 %collective-permute-start.1 = (bf16[2,2,64,1,288]{4,1,3,0,2:T(2,128)(2,1)S(1)}, bf16[2,2,64,1,288]{4,1,3,0,2:T(2,128)(2,1)S(1)}, u32[]{:S(2)}, u32[]{:S(2)}) collective-permute-start(bf16[2,2,64,1,288]{4,1,3,0,2:T(2,128)(2,1)S(1)} %fusion.6), channel_id=1, source_target_pairs={{1,0},{2,1},{3,2},{4,3},{5,4},{6,5},{7,6},{8,7},{9,8},{10,9},{11,1... | collective-permute-start | bytes 442376 | tf_op jit(solution)/shard_map/ppermute | solution.py:19
  150.5 17.3 %all-to-all-start.1 = ((bf16[2,2,64,3,288]{4,1,3,0,2:T(2,128)(2,1)}), bf16[2,2,64,3,288]{4,1,3,0,2:T(2,128)(2,1)S(1)}, u32[]{:S(2)}, u32[]{:S(2)}) async-start(bf16[2,2,64,3,288]{4,1,3,0,2:T(2,128)(2,1)} %pad_maximum_fusion), calls=%async_computation.1 | async-start | bytes 1179648 | tf_op jit(solution)/shard_map/all_to_all | solution.py:91
  170.6 0.6 copy-start.1
  174.2 17.9 %copy-start.2 = (bf16[2,1,2,1,96,96]{4,5,0,2,3,1:T(8,128)(2,1)}, bf16[2,1,2,1,96,96]{4,5,0,2,3,1:T(8,128)(2,1)S(1)}, u32[]{:S(2)}) copy-start(bf16[2,1,2,1,96,96]{4,5,0,2,3,1:T(8,128)(2,1)S(1)} %copy.163) | copy-start | bytes 221188
where the time goes:
time: 206 us; the launch traced here: 202 us
  local copies, waits for them, and re-layouts  116 us (56%)
  starting transfers between devices  33.1 us (16%)
  waiting for transfers between devices  30.2 us (15%)
  matrix products  15.7 us (8%)
  other arithmetic  6.03 us (3%)
    unnamed x21, local copies, waits for them, and re-layouts  82.3 us
    all_to_all x1, local copies, waits for them, and re-layouts, shards(): lax.all_to_all(local, 'energy', split_axis=3, concat_axis=2, tiled=True)  20.9 us
    all_to_all x1, starting transfers between devices, shards(): lax.all_to_all(local, 'energy', split_axis=3, concat_axis=2, tiled=True)  20.2 us
    all_to_all x1, waiting for transfers between devices, shards(): lax.all_to_all(bordered_entries, 'energy', split_axis=2, concat_axis=4, t...  11.6 us
    ppermute x1, waiting for transfers between devices, with_halo(): lax.ppermute(head, axis, [((i + 1) % count, i) for i in range(ends)])  11.1 us
    dot_general x12, matrix products, window_product(): jnp.einsum('gepq,epa->geqa', part, right, preferred_element_type=jnp.floa...  7.4 us
    all_to_all x1, waiting for transfers between devices, shards(): lax.all_to_all(local, 'energy', split_axis=3, concat_axis=2, tiled=True)  6.99 us
    ppermute x1, starting transfers between devices, with_halo(): lax.ppermute(tail, axis, [(i, (i + 1) % count) for i in range(ends)])  6.93 us
  transfers between devices with their start and end apart: 4, of which 4 were waited for; matrix products, arithmetic and copies ran while one was open for 2% of the time, Pallas kernels for 0%

commit v1 on v0

v1 whole, which is shorter than its diff:
```python
import functools
import math

import jax
import jax.numpy as jnp
import numpy as np
from jax import lax
from jax.experimental import pallas as pl
from jax.experimental.pallas import tpu as pltpu
from jax.sharding import PartitionSpec as P

MESH = pl.DeviceIdType.MESH
LANES = 128


def phase_tables(total):
    turns = np.outer(np.arange(total), np.arange(total)) % total
    angle = 2.0 * math.pi / total * turns
    parts = []
    for exact in (np.cos(angle), np.sin(angle)):
        high = exact.astype(jnp.bfloat16)
        low = (exact - high.astype(np.float64)).astype(jnp.bfloat16)
        parts.append((high, low))
    stacked = np.stack([parts[0][0], parts[1][0], parts[0][1], parts[1][1]])
    return np.tile(stacked, (1, 1, 4))


def dot(left, right):
    return jnp.dot(left, right, preferred_element_type=jnp.float32)


def iota(shape, axis):
    return lax.broadcasted_iota(jnp.int32, shape, axis)


def kernel(
    green, screened, retarded, order, start, tables, out,
    green_v, screen_v, own_v, order_v, start_v, tables_v,
    flat, chunks, land_one, weights, forward, backward,
    chunks_two, land_two, rows_two, from_left, from_right, right_side, spread, halo_out, halo_in,
    local_sem, send_one, recv_one, send_two, recv_two, ret_send, ret_recv, halo_send, halo_recv,
):
    n_e = lax.axis_size("energy")
    n_r = lax.axis_size("rows")
    me = lax.axis_index("energy")
    row = lax.axis_index("rows")
    slab, width = own_v.shape[2], own_v.shape[3]
    total = order_v.shape[1]
    per = slab // n_e
    has_left = row > 0
    has_right = row < n_r - 1

    barrier = pltpu.get_barrier_semaphore()

    @pl.loop(1, n_e)
    def _(step):
        pl.semaphore_signal(
            barrier, inc=1, device_id={"energy": lax.rem(me + step, n_e)}, device_id_type=MESH
        )

    @pl.when(has_left)
    def _():
        pl.semaphore_signal(barrier, inc=1, device_id={"rows": row - 1}, device_id_type=MESH)

    @pl.when(has_right)
    def _():
        pl.semaphore_signal(barrier, inc=1, device_id={"rows": row + 1}, device_id_type=MESH)

    loads = [
        pltpu.make_async_copy(green, green_v, local_sem.at[0]),
        pltpu.make_async_copy(order, order_v, local_sem.at[1]),
        pltpu.make_async_copy(tables, tables_v, local_sem.at[2]),
        pltpu.make_async_copy(screened, screen_v, local_sem.at[3]),
        pltpu.make_async_copy(retarded.at[:, :, 1], own_v, local_sem.at[4]),
        pltpu.make_async_copy(start, start_v, local_sem.at[5]),
    ]
    for load in loads:
        load.start()

    loads[0].wait()
    for pair in range(4):
        flat[2 * pair : 2 * pair + 2, :] = green_v[pair].astype(jnp.float32)
    group = n_e
    for size in (1, 2, 4, 8, 16):
        if size < n_e and n_e % size == 0 and size * per * slab % LANES == 0:
            group = size
            break
    margin = jnp.zeros((8, LANES - slab), jnp.float32)

    @pl.loop(0, n_e // group)
    def _(step):
        window = group * per * slab
        if group == n_e:
            cut = flat[...]
        else:
            cut = flat[:, pl.ds(pl.multiple_of(step * window, LANES), window)]
        for place in range(group * per):
            piece = cut[:, place * slab : (place + 1) * slab]
            lane = place % per * LANES
            chunks[step * group + place // per, :, lane : lane + LANES] = jnp.concatenate(
                [piece, margin], axis=1
            ).astype(jnp.bfloat16)

    beside = (row + n_r - 1) // n_r + (2 * n_r - 2 - row) // n_r
    pl.semaphore_wait(barrier, n_e - 1 + beside)

    def exchange(source, target, send_sem, recv_sem, step):
        other = lax.rem(me + step, n_e)
        return pltpu.make_async_remote_copy(
            src_ref=source.at[other],
            dst_ref=target.at[me],
            send_sem=send_sem.at[step],
            recv_sem=recv_sem.at[me],
            device_id={"energy": other},
            device_id_type=MESH,
        )

    def arrival(source, target, send_sem, recv_sem, step):
        other = lax.rem(me + step, n_e)
        return pltpu.make_async_remote_copy(
            src_ref=source.at[other],
            dst_ref=target.at[other],
            send_sem=send_sem.at[step],
            recv_sem=recv_sem.at[other],
            device_id={"energy": other},
            device_id_type=MESH,
        )

    one = (chunks, land_one, send_one, recv_one)
    two = (chunks_two, land_two, send_two, recv_two)

    @pl.loop(1, n_e)
    def _(step):
        exchange(*one, step).start()

    to_right = pltpu.make_async_remote_copy(
        src_ref=retarded.at[:, :, 2], dst_ref=from_left, send_sem=ret_send.at[0], recv_sem=ret_recv.at[0],
        device_id={"rows": lax.rem(row + 1, n_r)}, device_id_type=MESH,
    )
    to_left = pltpu.make_async_remote_copy(
        src_ref=retarded.at[:, :, 0], dst_ref=from_right, send_sem=ret_send.at[1], recv_sem=ret_recv.at[1],
        device_id={"rows": lax.rem(row + n_r - 1, n_r)}, device_id_type=MESH,
    )

    @pl.when(has_right)
    def _():
        to_right.start()

    @pl.when(has_left)
    def _():
        to_left.start()

    land_one[me] = chunks[me]

    loads[1].wait()
    loads[2].wait()
    count = 4 * total
    energies = (iota((total, total), 0) == order_v[...]).astype(jnp.bfloat16)
    column = iota((total, count), 1)
    slot_of_column = column // 8 * 2 + column % 2
    pick = (iota((total, count), 0) == slot_of_column).astype(jnp.bfloat16)
    hot = dot(energies, pick).astype(jnp.bfloat16)
    shape = (total, count)
    col = iota(shape, 1)
    col_g, col_c = col // 4 % 2, col // 2 % 2
    for part in range(2):
        cosine = dot(tables_v[2 * part, :, :total], hot)
        sine = dot(tables_v[2 * part + 1, :, :total], hot)
        for g in range(2):
            real = jnp.where(col_c == 0, cosine, sine)
            imag = jnp.where(col_c == 0, -sine, cosine)
            base = part * count + g * 2 * total
            forward[base : base + total, :] = jnp.where(col_g == g, real, 0.0).astype(jnp.bfloat16)
            forward[base + total : base + 2 * total, :] = jnp.where(col_g == g, imag, 0.0).astype(jnp.bfloat16)
    half = 2 * total
    line = iota((half, total), 0)
    slot_of_line = line // 4 * 2 + line % 2
    pick_line = (iota((half, total), 1) == slot_of_line).astype(jnp.bfloat16)
    hot_line = lax.dot_general(
        pick_line, energies, (((1,), (1,)), ((), ())), preferred_element_type=jnp.float32
    ).astype(jnp.bfloat16)
    shape = (half, count)
    same_g = iota(shape, 0) // 2 % 2 == iota(shape, 1) // (2 * total)
    from_real = iota(shape, 1) // total % 2 == 0
    scale = 1.0 / total
    for part in range(2):
        cosine = dot(hot_line, tables_v[2 * part]) * scale
        sine = dot(hot_line, tables_v[2 * part + 1]) * scale
        real = jnp.where(from_real, -sine, -cosine)
        imag = jnp.where(from_real, cosine, -sine)
        base = part * count
        backward[base : base + half, :] = jnp.where(same_g, real, 0.0).astype(jnp.bfloat16)
        backward[base + half : base + count, :] = jnp.where(same_g, imag, 0.0).astype(jnp.bfloat16)

    loads[3].wait()
    screen_margin = jnp.zeros((total, LANES - slab), jnp.float32)
    for pair in range(4):
        entries = screen_v[pair].astype(jnp.float32)
        for p in range(per):
            weights[pair * total : (pair + 1) * total, p * LANES : (p + 1) * LANES] = jnp.concatenate(
                [entries[:, p * slab : (p + 1) * slab], screen_margin], axis=1
            )

    lines = 4 * n_e
    line = iota((lines, slab), 0)
    orbital = iota((lines, slab), 1)
    blank = jnp.zeros((LANES - slab, width), jnp.bfloat16)

    def prepare(block, target):
        for slot in range(2):
            real = block[0, slot]
            imag = block[1, slot]
            for side, (upper, lower) in enumerate(((real, imag), (-imag, real))):
                right_side[target, slot, side, 0:slab] = upper
                right_side[target, slot, side, slab:LANES] = blank
                right_side[target, slot, side, LANES : LANES + slab] = lower
                right_side[target, slot, side, LANES + slab :] = blank
            for p in range(per):
                chosen = jnp.where(line % 2 == slot, line // 4 * per + p, -1)
                select = (orbital == chosen).astype(jnp.bfloat16)
                spread[target, slot, 0, p] = dot(select, real)
                spread[target, slot, 1, p] = dot(select, imag)

    loads[4].wait()
    prepare(own_v, 2)

    @pl.loop(1, n_e)
    def _(step):
        arrival(*one, step).wait_recv()

    arrived = land_one[...].reshape(8 * n_e, per * LANES)
    times = dot(forward[...], arrived)
    times = times[:count] + times[count:]
    mixed = []
    for g in range(2):
        base = g * 2 * total
        green_re, green_im = times[base : base + total], times[base + total : base + 2 * total]
        screen_re, screen_im = weights[base : base + total], weights[base + total : base + 2 * total]
        mixed.append(green_re * screen_re - green_im * screen_im)
        mixed.append(green_re * screen_im + green_im * screen_re)
    mixed = jnp.concatenate(mixed, axis=0)
    high = mixed.astype(jnp.bfloat16)
    low = (mixed - high.astype(jnp.float32)).astype(jnp.bfloat16)
    first = dot(backward[...], high)
    sigma = first[:count] + (first[count:] + dot(backward[0:count], low))
    sigma = sigma.astype(jnp.bfloat16)
    for c in range(2):
        for p in range(per):
            lane = (2 * p + c) * LANES
            chunks_two[:, :, lane : lane + LANES] = sigma[
                c * half : (c + 1) * half, p * LANES : (p + 1) * LANES
            ].reshape(n_e, 4, LANES)

    @pl.loop(1, n_e)
    def _(step):
        exchange(*two, step).start()

    land_two[me] = chunks_two[me]

    @pl.when(has_left)
    def _():
        to_right.wait_recv()
        prepare(from_left, 0)

    @pl.when(has_right)
    def _():
        to_left.wait_recv()
        prepare(from_right, 1)

    loads[5].wait()

    @pl.loop(1, n_e)
    def _(step):
        arrival(*two, step).wait_recv()

    for p in range(per):
        rows_two[p] = land_two[:, :, 2 * p * LANES : 2 * (p + 1) * LANES].reshape(lines, 2 * LANES)

    def fold(values):
        values = values.reshape(lines // 8, 8, values.shape[1]).sum(axis=0)
        return values[0:4] + values[4:8]

    def contribution(target):
        real = jnp.zeros((4, width), jnp.float32)
        imag = jnp.zeros((4, width), jnp.float32)
        for p in range(per):
            for slot in range(2):
                inner_re = dot(rows_two[p], right_side[target, slot, 0])
                inner_im = dot(rows_two[p], right_side[target, slot, 1])
                outer_re = spread[target, slot, 0, p]
                outer_im = spread[target, slot, 1, p]
                real = real + fold(outer_re * inner_re - outer_im * inner_im)
                imag = imag + fold(outer_re * inner_im + outer_im * inner_re)
        return jnp.concatenate([real, imag], axis=0)

    back_left = pltpu.make_async_remote_copy(
        src_ref=halo_out.at[0], dst_ref=halo_in.at[1], send_sem=halo_send.at[0], recv_sem=halo_recv.at[1],
        device_id={"rows": lax.rem(row + n_r - 1, n_r)}, device_id_type=MESH,
    )
    back_right = pltpu.make_async_remote_copy(
        src_ref=halo_out.at[1], dst_ref=halo_in.at[0], send_sem=halo_send.at[1], recv_sem=halo_recv.at[0],
        device_id={"rows": lax.rem(row + 1, n_r)}, device_id_type=MESH,
    )

    @pl.when(row == 0)
    def _():
        halo_in[0] = jnp.zeros(halo_in.shape[1:], jnp.float32)

    @pl.when(row == n_r - 1)
    def _():
        halo_in[1] = jnp.zeros(halo_in.shape[1:], jnp.float32)

    @pl.when(has_left)
    def _():
        halo_out[0] = contribution(0)
        back_left.start()

    @pl.when(has_right)
    def _():
        halo_out[1] = contribution(1)
        back_right.start()

    density = contribution(2)
    direct = [jnp.zeros((4, LANES), jnp.float32), jnp.zeros((4, LANES), jnp.float32)]
    shape = (lines, LANES)
    for p in range(per):
        on_diagonal = iota(shape, 1) == iota(shape, 0) // 4 * per + p
        for c in range(2):
            entries = rows_two[p, :, c * LANES : (c + 1) * LANES].astype(jnp.float32)
            direct[c] = direct[c] + fold(jnp.where(on_diagonal, entries, 0.0))
    shape = (LANES, width)
    place = iota(shape, 1) == iota(shape, 0) + start_v[0]
    density = density + dot(
        jnp.concatenate(direct, axis=0).astype(jnp.bfloat16), place.astype(jnp.bfloat16)
    )

    @pl.when(has_left)
    def _():
        back_right.wait_recv()

    @pl.when(has_right)
    def _():
        back_left.wait_recv()

    density = density + halo_in[0] + halo_in[1]
    for c in range(2):
        for g in range(2):
            out[g, c] = density[4 * c + 2 * g : 4 * c + 2 * g + 2]

    @pl.loop(1, n_e)
    def _(step):
        exchange(*one, step).wait_send()
        exchange(*two, step).wait_send()

    @pl.when(has_right)
    def _():
        to_right.wait_send()
        back_right.wait_send()

    @pl.when(has_left)
    def _():
        to_left.wait_send()
        back_left.wait_send()


def shards(green_window, screened, retarded, energy_order, window_start):
    n_e = lax.axis_size("energy")
    entries = green_window.shape[4]
    columns = screened.shape[4]
    total = screened.shape[2]
    slab, width = retarded.shape[4], retarded.shape[5]
    per = slab // n_e
    half = jnp.bfloat16
    full = jnp.float32
    lines = 4 * n_e
    scratch = [
        pltpu.VMEM((4, 2, entries), half),
        pltpu.VMEM((4, total, columns), half),
        pltpu.VMEM((2, 2, slab, width), half),
        pltpu.VMEM((1, total), jnp.int32),
        pltpu.SMEM((1,), jnp.int32),
        pltpu.VMEM((4, total, 4 * total), half),
        pltpu.VMEM((8, entries), full),
        pltpu.VMEM((n_e, 8, per * LANES), half),
        pltpu.VMEM((n_e, 8, per * LANES), half),
        pltpu.VMEM((4 * total, per * LANES), full),
        pltpu.VMEM((8 * total, 4 * total), half),
        pltpu.VMEM((8 * total, 4 * total), half),
        pltpu.VMEM((n_e, 4, 2 * per * LANES), half),
        pltpu.VMEM((n_e, 4, 2 * per * LANES), half),
        pltpu.VMEM((per, lines, 2 * LANES), half),
        pltpu.VMEM((2, 2, slab, width), half),
        pltpu.VMEM((2, 2, slab, width), half),
        pltpu.VMEM((3, 2, 2, 2 * LANES, width), half),
        pltpu.VMEM((3, 2, 2, per, lines, width), full),
        pltpu.VMEM((2, 8, width), full),
        pltpu.VMEM((2, 8, width), full),
        pltpu.SemaphoreType.DMA((6,)),
        pltpu.SemaphoreType.DMA((n_e,)),
        pltpu.SemaphoreType.DMA((n_e,)),
        pltpu.SemaphoreType.DMA((n_e,)),
        pltpu.SemaphoreType.DMA((n_e,)),
        pltpu.SemaphoreType.DMA((2,)),
        pltpu.SemaphoreType.DMA((2,)),
        pltpu.SemaphoreType.DMA((2,)),
        pltpu.SemaphoreType.DMA((2,)),
    ]
    anywhere = pl.BlockSpec(memory_space=pl.ANY)
    density = pl.pallas_call(
        kernel,
        out_shape=jax.ShapeDtypeStruct((2, 2, 2, width), full),
        in_specs=[anywhere] * 6,
        out_specs=pl.BlockSpec(memory_space=pltpu.VMEM),
        scratch_shapes=scratch,
        compiler_params=pltpu.CompilerParams(
            collective_id=0, has_side_effects=True, vmem_limit_bytes=48 * 2**20
        ),
    )(
        green_window.reshape(4, 2, entries),
        screened.reshape(4, total, columns),
        retarded[:, :, 0],
        energy_order.reshape(1, total),
        window_start,
        jnp.asarray(phase_tables(total)),
    )
    return density[:, :, :, None, :]


def solution(mesh):
    in_specs = (
        P(None, None, "energy", "rows", None),
        P(None, None, None, "rows", "energy"),
        P(None, "energy", "rows", None, None, None),
        P(),
        P("rows"),
    )
    out_specs = P(None, None, "energy", "rows", None)
    return jax.shard_map(shards, mesh=mesh, in_specs=in_specs, out_specs=out_specs, check_vma=False)
```

time: 206 us -> 49.1 us (0.24); the launches traced: 202 us -> 48.9 us
  local copies, waits for them, and re-layouts: 116 us -> 5.06 us
  Pallas kernels: 0 us -> 43.1 us
  starting transfers between devices: 33.1 us -> 0 us
  waiting for transfers between devices: 30.2 us -> 0 us
  matrix products: 15.7 us -> 0 us
  other arithmetic: 6.03 us -> 0 us
    unnamed x21 -> x10, local copies, waits for them, and re-layouts: 82.3 us -> 4.45 us
    pallas_call x0 -> x1, Pallas kernels: none -> 43.1 us  [shards(): pl.pallas_call(kernel, out_shape=jax.ShapeDtypeStruct((2, 2, 2, width), f...]
    all_to_all x2 -> x0, starting transfers between devices: 24.1 us -> none  [the longest x1 20.2 us: shards(): lax.all_to_all(local, 'energy', split_axis=3, concat_axis=2, tiled=True)]
    all_to_all x2 -> x0, local copies, waits for them, and re-layouts: 20.9 us -> none  [the longest x1 20.9 us: shards(): lax.all_to_all(local, 'energy', split_axis=3, concat_axis=2, tiled=True)]
    all_to_all x2 -> x0, waiting for transfers between devices: 18.6 us -> none  [the longest x1 11.6 us: shards(): lax.all_to_all(bordered_entries, 'energy', split_axis=2, concat_axis=4, t...]
    dot_general x29 -> x0, matrix products: 15.7 us -> none  [the longest x12 7.4 us: window_product(): jnp.einsum('gepq,epa->geqa', part, right, preferred_element_type=jnp.floa...]
    ppermute x2 -> x0, waiting for transfers between devices: 11.6 us -> none  [the longest x1 11.1 us: with_halo(): lax.ppermute(head, axis, [((i + 1) % count, i) for i in range(ends)])]
    ppermute x2 -> x0, starting transfers between devices: 9.07 us -> none  [the longest x1 6.93 us: with_halo(): lax.ppermute(tail, axis, [(i, (i + 1) % count) for i in range(ends)])]
  transfers between devices with their start and end apart: 4 -> 0, of which waited for: 4 -> 0; matrix products, arithmetic and copies ran while one was open for 2% -> 0% of each run, Pallas kernels for 0% -> 0%
where the time goes in v1:
time: 49.1 us; the launch traced here: 48.9 us
  Pallas kernels  43.1 us (88%)
  local copies, waits for them, and re-layouts  5.06 us (10%)
  between operations  0.67 us (1%)
    pallas_call x1, Pallas kernels, shards(): pl.pallas_call(kernel, out_shape=jax.ShapeDtypeStruct((2, 2, 2, width), f...  43.1 us
    unnamed x10, local copies, waits for them, and re-layouts  4.45 us

profile of v1, /device:TPU:15, one launch (start us, length us, event | category | flops | bytes accessed | tf_op | source)
XLA Modules:
  0.0 48.9 jit_solution(1373362635490774784)
XLA Ops:
  0.7 0.0 copy-start.4
  0.7 0.6 %copy-done.4 = s32[64]{0:T(128)S(1)} copy-done((s32[64]{0:T(128)S(1)}, s32[64]{0:T(128)}, u32[]{:S(2)}) %copy-start.4) | copy-done | bytes 280
  1.3 0.0 copy-start
  1.3 1.1 %copy-done = bf16[2,2,1,3,96,192]{5,4,3,2,1,0:T(8,128)(2,1)S(1)} copy-done((bf16[2,2,1,3,96,192]{5,4,3,2,1,0:T(8,128)(2,1)S(1)}, bf16[2,2,1,3,96,192]{5,4,3,2,1,0:T(8,128)(2,1)}, u32[]{:S(2)}) %copy-start) | copy-done | bytes 442392
  2.4 0.0 copy-start.1
  2.4 0.9 %copy-done.1 = bf16[2,2,64,1,288]{4,2,3,1,0:T(8,128)(2,1)S(1)} copy-done((bf16[2,2,64,1,288]{4,2,3,1,0:T(8,128)(2,1)S(1)}, bf16[2,2,64,1,288]{4,2,3,1,0:T(8,128)(2,1)}, u32[]{:S(2)}) %copy-start.1) | copy-done | bytes 147480
  3.3 0.0 copy-start.2
  3.3 0.9 %copy-done.2 = bf16[2,2,2,1,9216]{4,2,3,1,0:T(2,128)(2,1)S(1)} copy-done((bf16[2,2,2,1,9216]{4,2,3,1,0:T(2,128)(2,1)S(1)}, bf16[2,2,2,1,9216]{4,2,3,1,0:T(2,128)(2,1)}, u32[]{:S(2)}) %copy-start.2) | copy-done | bytes 147480
  4.2 0.0 copy-start.3
  4.2 0.9 %copy-done.3 = bf16[4,64,256]{2,1,0:T(8,128)(2,1)S(1)} copy-done((bf16[4,64,256]{2,1,0:T(8,128)(2,1)S(1)}, bf16[4,64,256]{2,1,0:T(8,128)(2,1)}, u32[]{:S(2)}) %copy-start.3) | copy-done | bytes 131096
  5.1 43.1 %shard_map.64 = f32[2,2,2,192]{3,2,1,0:T(2,128)S(1)} custom-call(bf16[4,2,9216]{2,1,0:T(2,128)(2,1)S(1)} %bitcast.7, bf16[4,64,288]{2,1,0:T(8,128)(2,1)S(1)} %bitcast.6, bf16[2,2,3,96,192]{4,3,2,1,0:T(8,128)(2,1)S(1)} %bitcast.5, s32[1,64]{1,0:T(1,128)S(1)} %bitcast.9, s32[1]{0:T(128)S(6)} %copy.8.start, bf16[4,64,256]{2,1,0:T(8,128)(2,1)S(1)} %copy-done.3), custom_call_target="tpu_custom_call" | custom-call | tf_op jit(solution)/shard_map/pallas_call | solution.py:409
  48.3 0.6 %copy.7 = f32[2,2,2,1,192]{4,3,2,1,0:T(1,128)} copy(f32[2,2,2,1,192]{4,2,1,0,3:T(2,128)S(1)} %bitcast.8) | data formatting | bytes 12288 | tf_op jit(solution)/shard_map/broadcast_in_dim | solution.py:426
Async XLA Ops:
  0.7 0.7 %copy-start.4 = (s32[64]{0:T(128)S(1)}, s32[64]{0:T(128)}, u32[]{:S(2)}) copy-start(s32[64]{0:T(128)} %param.9) | copy-start | bytes 772
  1.3 1.1 %copy-start = (bf16[2,2,1,3,96,192]{5,4,3,2,1,0:T(8,128)(2,1)S(1)}, bf16[2,2,1,3,96,192]{5,4,3,2,1,0:T(8,128)(2,1)}, u32[]{:S(2)}) copy-start(bf16[2,2,1,3,96,192]{5,4,3,2,1,0:T(8,128)(2,1)} %param.8) | copy-start | bytes 1327108
  2.4 0.9 %copy-start.1 = (bf16[2,2,64,1,288]{4,2,3,1,0:T(8,128)(2,1)S(1)}, bf16[2,2,64,1,288]{4,2,3,1,0:T(8,128)(2,1)}, u32[]{:S(2)}) copy-start(bf16[2,2,64,1,288]{4,2,3,1,0:T(8,128)(2,1)} %param.7) | copy-start | bytes 442372
  3.3 0.9 %copy-start.2 = (bf16[2,2,2,1,9216]{4,2,3,1,0:T(2,128)(2,1)S(1)}, bf16[2,2,2,1,9216]{4,2,3,1,0:T(2,128)(2,1)}, u32[]{:S(2)}) copy-start(bf16[2,2,2,1,9216]{4,2,3,1,0:T(2,128)(2,1)} %param.6) | copy-start | bytes 442372
  4.2 0.9 %copy-start.3 = (bf16[4,64,256]{2,1,0:T(8,128)(2,1)S(1)}, bf16[4,64,256]{2,1,0:T(8,128)(2,1)}, u32[]{:S(2)}) copy-start(bf16[4,64,256]{2,1,0:T(8,128)(2,1)} %constant.2.clone.tables) | copy-start | bytes 393220

commit v2 on v1

--- a/solution.py
+++ b/solution.py
@@ -37,8 +37,8 @@
     green, screened, retarded, order, start, tables, out,
     green_v, screen_v, own_v, order_v, start_v, tables_v,
     flat, chunks, land_one, weights, forward, backward,
-    chunks_two, land_two, rows_two, from_left, from_right, right_side, spread, halo_out, halo_in,
-    local_sem, send_one, recv_one, send_two, recv_two, ret_send, ret_recv, halo_send, halo_recv,
+    chunks_two, land_two, rows_two, land_far, rows_far, far_v, from_left, from_right, right_side, spread, halo_out, halo_in,
+    local_sem, send_one, recv_one, send_two, recv_two, send_far, recv_far, ret_send, ret_recv, halo_send, halo_recv,
 ):
     n_e = lax.axis_size("energy")
     n_r = lax.axis_size("rows")
@@ -47,8 +47,12 @@
     slab, width = own_v.shape[2], own_v.shape[3]
     total = order_v.shape[1]
     per = slab // n_e
-    has_left = row > 0
-    has_right = row < n_r - 1
+    middle = n_r // 2
+    far_row = 2 * middle - 1 - row
+    far_side = middle - row
+    is_far = jnp.logical_or(row == middle - 1, row == middle)
+    has_left = jnp.logical_and(row > 0, row != middle)
+    has_right = jnp.logical_and(row < n_r - 1, row != middle - 1)
 
     barrier = pltpu.get_barrier_semaphore()
 
@@ -58,11 +62,11 @@
             barrier, inc=1, device_id={"energy": lax.rem(me + step, n_e)}, device_id_type=MESH
         )
 
-    @pl.when(has_left)
+    @pl.when(row > 0)
     def _():
         pl.semaphore_signal(barrier, inc=1, device_id={"rows": row - 1}, device_id_type=MESH)
 
-    @pl.when(has_right)
+    @pl.when(row < n_r - 1)
     def _():
         pl.semaphore_signal(barrier, inc=1, device_id={"rows": row + 1}, device_id_type=MESH)
 
@@ -76,6 +80,11 @@
     ]
     for load in loads:
         load.start()
+    far_load = pltpu.make_async_copy(retarded.at[:, :, 2 * far_side], far_v, local_sem.at[6])
+
+    @pl.when(is_far)
+    def _():
+        far_load.start()
 
     loads[0].wait()
     for pair in range(4):
@@ -123,6 +132,16 @@
             send_sem=send_sem.at[step],
             recv_sem=recv_sem.at[other],
             device_id={"energy": other},
+            device_id_type=MESH,
+        )
+
+    def cross(step, device):
+        return pltpu.make_async_remote_copy(
+            src_ref=chunks_two.at[step],
+            dst_ref=land_far.at[device],
+            send_sem=send_far.at[step],
+            recv_sem=recv_far.at[device],
+            device_id={"energy": step, "rows": far_row},
             device_id_type=MESH,
         )
 
@@ -224,6 +243,11 @@
     loads[4].wait()
     prepare(own_v, 2)
 
+    @pl.when(is_far)
+    def _():
+        far_load.wait()
+        prepare(far_v, far_side)
+
     @pl.loop(1, n_e)
     def _(step):
         arrival(*one, step).wait_recv()
@@ -255,6 +279,12 @@
     def _(step):
         exchange(*two, step).start()
 
+    @pl.when(is_far)
+    def _():
+        @pl.loop(0, n_e)
+        def _(step):
+            cross(lax.rem(me + step, n_e), me).start()
+
     land_two[me] = chunks_two[me]
 
     @pl.when(has_left)
@@ -273,20 +303,23 @@
     def _(step):
         arrival(*two, step).wait_recv()
 
-    for p in range(per):
-        rows_two[p] = land_two[:, :, 2 * p * LANES : 2 * (p + 1) * LANES].reshape(lines, 2 * LANES)
+    def regroup(landed, grouped):
+        for p in range(per):
+            grouped[p] = landed[:, :, 2 * p * LANES : 2 * (p + 1) * LANES].reshape(lines, 2 * LANES)
+
+    regroup(land_two, rows_two)
 
     def fold(values):
         values = values.reshape(lines // 8, 8, values.shape[1]).sum(axis=0)
         return values[0:4] + values[4:8]
 
-    def contribution(target):
+    def contribution(target, grouped):
         real = jnp.zeros((4, width), jnp.float32)
         imag = jnp.zeros((4, width), jnp.float32)
         for p in range(per):
             for slot in range(2):
-                inner_re = dot(rows_two[p], right_side[target, slot, 0])
-                inner_im = dot(rows_two[p], right_side[target, slot, 1])
+                inner_re = dot(grouped[p], right_side[target, slot, 0])
+                inner_im = dot(grouped[p], right_side[target, slot, 1])
                 outer_re = spread[target, slot, 0, p]
                 outer_im = spread[target, slot, 1, p]
                 real = real + fold(outer_re * inner_re - outer_im * inner_im)
@@ -302,25 +335,25 @@
         device_id={"rows": lax.rem(row + 1, n_r)}, device_id_type=MESH,
     )
 
-    @pl.when(row == 0)
+    @pl.when(jnp.logical_not(has_left))
     def _():
         halo_in[0] = jnp.zeros(halo_in.shape[1:], jnp.float32)
 
-    @pl.when(row == n_r - 1)
+    @pl.when(jnp.logical_not(has_right))
     def _():
         halo_in[1] = jnp.zeros(halo_in.shape[1:], jnp.float32)
 
     @pl.when(has_left)
     def _():
-        halo_out[0] = contribution(0)
+        halo_out[0] = contribution(0, rows_two)
         back_left.start()
 
     @pl.when(has_right)
     def _():
-        halo_out[1] = contribution(1)
+        halo_out[1] = contribution(1, rows_two)
         back_right.start()
 
-    density = contribution(2)
+    density = contribution(2, rows_two)
     direct = [jnp.zeros((4, LANES), jnp.float32), jnp.zeros((4, LANES), jnp.float32)]
     shape = (lines, LANES)
     for p in range(per):
@@ -329,10 +362,19 @@
             entries = rows_two[p, :, c * LANES : (c + 1) * LANES].astype(jnp.float32)
             direct[c] = direct[c] + fold(jnp.where(on_diagonal, entries, 0.0))
     shape = (LANES, width)
-    place = iota(shape, 1) == iota(shape, 0) + start_v[0]
+    place = iota(shape, 1) == iota(shape, 0) + start_v[...]
     density = density + dot(
         jnp.concatenate(direct, axis=0).astype(jnp.bfloat16), place.astype(jnp.bfloat16)
     )
+
+    @pl.when(is_far)
+    def _():
+        @pl.loop(0, n_e)
+        def _(step):
+            cross(step, step).wait_recv()
+
+        regroup(land_far, rows_far)
+        halo_in[far_side] = contribution(far_side, rows_far)
 
     @pl.when(has_left)
     def _():
@@ -351,6 +393,12 @@
     def _(step):
         exchange(*one, step).wait_send()
         exchange(*two, step).wait_send()
+
+    @pl.when(is_far)
+    def _():
+        @pl.loop(0, n_e)
+        def _(step):
+            cross(step, me).wait_send()
 
     @pl.when(has_right)
     def _():
@@ -378,7 +426,7 @@
         pltpu.VMEM((4, total, columns), half),
         pltpu.VMEM((2, 2, slab, width), half),
         pltpu.VMEM((1, total), jnp.int32),
-        pltpu.SMEM((1,), jnp.int32),
+        pltpu.VMEM((1, 1), jnp.int32),
         pltpu.VMEM((4, total, 4 * total), half),
         pltpu.VMEM((8, entries), full),
         pltpu.VMEM((n_e, 8, per * LANES), half),
@@ -389,13 +437,18 @@
         pltpu.VMEM((n_e, 4, 2 * per * LANES), half),
         pltpu.VMEM((n_e, 4, 2 * per * LANES), half),
         pltpu.VMEM((per, lines, 2 * LANES), half),
+        pltpu.VMEM((n_e, 4, 2 * per * LANES), half),
+        pltpu.VMEM((per, lines, 2 * LANES), half),
+        pltpu.VMEM((2, 2, slab, width), half),
         pltpu.VMEM((2, 2, slab, width), half),
         pltpu.VMEM((2, 2, slab, width), half),
         pltpu.VMEM((3, 2, 2, 2 * LANES, width), half),
         pltpu.VMEM((3, 2, 2, per, lines, width), full),
         pltpu.VMEM((2, 8, width), full),
         pltpu.VMEM((2, 8, width), full),
-        pltpu.SemaphoreType.DMA((6,)),
+        pltpu.SemaphoreType.DMA((7,)),
+        pltpu.SemaphoreType.DMA((n_e,)),
+        pltpu.SemaphoreType.DMA((n_e,)),
         pltpu.SemaphoreType.DMA((n_e,)),
         pltpu.SemaphoreType.DMA((n_e,)),
         pltpu.SemaphoreType.DMA((n_e,)),
@@ -405,7 +458,7 @@
         pltpu.SemaphoreType.DMA((2,)),
         pltpu.SemaphoreType.DMA((2,)),
     ]
-    anywhere = pl.BlockSpec(memory_space=pl.ANY)
+    anywhere = pl.BlockSpec(memory_space=pltpu.HBM)
     density = pl.pallas_call(
         kernel,
         out_shape=jax.ShapeDtypeStruct((2, 2, 2, width), full),
@@ -413,14 +466,14 @@
         out_specs=pl.BlockSpec(memory_space=pltpu.VMEM),
         scratch_shapes=scratch,
         compiler_params=pltpu.CompilerParams(
-            collective_id=0, has_side_effects=True, vmem_limit_bytes=48 * 2**20
+            collective_id=0, has_side_effects=True, vmem_limit_bytes=67043328
         ),
     )(
         green_window.reshape(4, 2, entries),
         screened.reshape(4, total, columns),
         retarded[:, :, 0],
         energy_order.reshape(1, total),
-        window_start,
+        window_start.reshape(1, 1),
         jnp.asarray(phase_tables(total)),
     )
     return density[:, :, :, None, :]

time: 49.1 us -> 44.4 us (0.904)
  local copies, waits for them, and re-layouts: 5.06 us -> 1.3 us
  Pallas kernels: 43.1 us -> 42.1 us
    unnamed x10 -> x0, local copies, waits for them, and re-layouts: 4.45 us -> none
    pallas_call x1, Pallas kernels: 43.1 us -> 42.1 us  [shards(): pl.pallas_call(kernel, out_shape=jax.ShapeDtypeStruct((2, 2, 2, width), f...]
    broadcast_in_dim x1, local copies, waits for them, and re-layouts: 0.61 us -> 1.3 us  [shards(): return density[:, :, :, None, :]]
where the time goes in v2:
time: 44.4 us; the launch traced here: 44.1 us
  Pallas kernels  42.1 us (95%)
  local copies, waits for them, and re-layouts  1.3 us (3%)
  between operations  0.66 us (1%)
    pallas_call x1, Pallas kernels, shards(): pl.pallas_call(kernel, out_shape=jax.ShapeDtypeStruct((2, 2, 2, width), f...  42.1 us
    broadcast_in_dim x1, local copies, waits for them, and re-layouts, shards(): return density[:, :, :, None, :]  1.3 us

profile of v2, /device:TPU:15, one launch (start us, length us, event | category | flops | bytes accessed | tf_op | source)
XLA Modules:
  0.0 44.1 jit_solution(2106291291231287524)
XLA Ops:
  0.7 42.1 %shard_map.64 = f32[2,2,2,192]{3,2,1,0:T(2,128)} custom-call(bf16[4,2,9216]{2,1,0:T(2,128)(2,1)} %bitcast.9, bf16[4,64,288]{2,1,0:T(8,128)(2,1)} %bitcast.8, bf16[2,2,3,96,192]{4,3,2,1,0:T(8,128)(2,1)} %bitcast.7, s32[1,64]{1,0:T(1,128)} %bitcast.11, s32[1,1]{1,0:T(1,128)} %bitcast.6.start, bf16[4,64,256]{2,1,0:T(8,128)(2,1)} %constant.2.clone.tables), custom_call_target="tpu_custom_call" | custom-call | tf_op jit(solution)/shard_map/pallas_call | solution.py:462
  42.8 1.3 %copy.7 = f32[2,2,2,1,192]{4,3,2,1,0:T(1,128)} copy(f32[2,2,2,1,192]{4,2,1,0,3:T(2,128)} %bitcast.10) | data formatting | bytes 12288 | tf_op jit(solution)/shard_map/broadcast_in_dim | solution.py:479

commit v3 on v2

--- a/solution.py
+++ b/solution.py
@@ -10,6 +10,7 @@
 from jax.sharding import PartitionSpec as P
 
 MESH = pl.DeviceIdType.MESH
+PLANES = 8
 LANES = 128
 
 
@@ -34,8 +35,8 @@
 
 
 def kernel(
-    green, screened, retarded, order, start, tables, out,
-    green_v, screen_v, own_v, order_v, start_v, tables_v,
+    green, screened, retarded, order, tables, start, out,
+    green_v, screen_v, own_v, order_v, tables_v,
     flat, chunks, land_one, weights, forward, backward,
     chunks_two, land_two, rows_two, land_far, rows_far, far_v, from_left, from_right, right_side, spread, halo_out, halo_in,
     local_sem, send_one, recv_one, send_two, recv_two, send_far, recv_far, ret_send, ret_recv, halo_send, halo_recv,
@@ -56,11 +57,13 @@
 
     barrier = pltpu.get_barrier_semaphore()
 
-    @pl.loop(1, n_e)
-    def _(step):
-        pl.semaphore_signal(
-            barrier, inc=1, device_id={"energy": lax.rem(me + step, n_e)}, device_id_type=MESH
-        )
+    @pl.loop(0, n_e)
+    def _(step):
+        other = lax.rem(me + 1 + step, n_e)
+
+        @pl.when(other != me)
+        def _():
+            pl.semaphore_signal(barrier, inc=1, device_id={"energy": other}, device_id_type=MESH)
 
     @pl.when(row > 0)
     def _():
@@ -76,7 +79,6 @@
         pltpu.make_async_copy(tables, tables_v, local_sem.at[2]),
         pltpu.make_async_copy(screened, screen_v, local_sem.at[3]),
         pltpu.make_async_copy(retarded.at[:, :, 1], own_v, local_sem.at[4]),
-        pltpu.make_async_copy(start, start_v, local_sem.at[5]),
     ]
     for load in loads:
         load.start()
@@ -113,23 +115,21 @@
     beside = (row + n_r - 1) // n_r + (2 * n_r - 2 - row) // n_r
     pl.semaphore_wait(barrier, n_e - 1 + beside)
 
-    def exchange(source, target, send_sem, recv_sem, step):
-        other = lax.rem(me + step, n_e)
+    def exchange(source, target, send_sem, recv_sem, other):
         return pltpu.make_async_remote_copy(
             src_ref=source.at[other],
             dst_ref=target.at[me],
-            send_sem=send_sem.at[step],
+            send_sem=send_sem.at[other],
             recv_sem=recv_sem.at[me],
             device_id={"energy": other},
             device_id_type=MESH,
         )
 
-    def arrival(source, target, send_sem, recv_sem, step):
-        other = lax.rem(me + step, n_e)
+    def arrival(source, target, send_sem, recv_sem, other):
         return pltpu.make_async_remote_copy(
             src_ref=source.at[other],
             dst_ref=target.at[other],
-            send_sem=send_sem.at[step],
+            send_sem=send_sem.at[other],
             recv_sem=recv_sem.at[other],
             device_id={"energy": other},
             device_id_type=MESH,
@@ -148,9 +148,13 @@
     one = (chunks, land_one, send_one, recv_one)
     two = (chunks_two, land_two, send_two, recv_two)
 
-    @pl.loop(1, n_e)
-    def _(step):
-        exchange(*one, step).start()
+    @pl.loop(0, n_e)
+    def _(step):
+        other = lax.rem(me + 1 + step, n_e)
+
+        @pl.when(other != me)
+        def _():
+            exchange(*one, other).start()
 
     to_right = pltpu.make_async_remote_copy(
         src_ref=retarded.at[:, :, 2], dst_ref=from_left, send_sem=ret_send.at[0], recv_sem=ret_recv.at[0],
@@ -237,8 +241,9 @@
             for p in range(per):
                 chosen = jnp.where(line % 2 == slot, line // 4 * per + p, -1)
                 select = (orbital == chosen).astype(jnp.bfloat16)
-                spread[target, slot, 0, p] = dot(select, real)
-                spread[target, slot, 1, p] = dot(select, imag)
+                for part, values in enumerate((real, imag)):
+                    rows = dot(select, values)
+                    spread[target, part, p] = rows if slot == 0 else spread[target, part, p] + rows
 
     loads[4].wait()
     prepare(own_v, 2)
@@ -250,7 +255,7 @@
 
     @pl.loop(1, n_e)
     def _(step):
-        arrival(*one, step).wait_recv()
+        arrival(*one, lax.rem(me + step, n_e)).wait_recv()
 
     arrived = land_one[...].reshape(8 * n_e, per * LANES)
     times = dot(forward[...], arrived)
@@ -275,15 +280,21 @@
                 c * half : (c + 1) * half, p * LANES : (p + 1) * LANES
             ].reshape(n_e, 4, LANES)
 
-    @pl.loop(1, n_e)
-    def _(step):
-        exchange(*two, step).start()
+    plane = max(1, n_e // PLANES)
+
+    @pl.loop(0, n_e)
+    def _(step):
+        other = step // plane * plane + lax.rem(me + step, plane)
+
+        @pl.when(other != me)
+        def _():
+            exchange(*two, other).start()
 
     @pl.when(is_far)
     def _():
         @pl.loop(0, n_e)
         def _(step):
-            cross(lax.rem(me + step, n_e), me).start()
+            cross(step // plane * plane + lax.rem(me + step, plane), me).start()
 
     land_two[me] = chunks_two[me]
 
@@ -297,11 +308,13 @@
         to_left.wait_recv()
         prepare(from_right, 1)
 
-    loads[5].wait()
-
     @pl.loop(1, n_e)
     def _(step):
-        arrival(*two, step).wait_recv()
+        exchange(*one, lax.rem(me + step, n_e)).wait_send()
+
+    @pl.loop(1, n_e)
+    def _(step):
+        arrival(*two, lax.rem(me + step, n_e)).wait_recv()
 
     def regroup(landed, grouped):
         for p in range(per):
@@ -312,28 +325,36 @@
     def fold(values):
         values = values.reshape(lines // 8, 8, values.shape[1]).sum(axis=0)
         return values[0:4] + values[4:8]
+
+    first_slot = iota((lines, width), 0) % 2 == 0
 
     def contribution(target, grouped):
         real = jnp.zeros((4, width), jnp.float32)
         imag = jnp.zeros((4, width), jnp.float32)
         for p in range(per):
-            for slot in range(2):
-                inner_re = dot(grouped[p], right_side[target, slot, 0])
-                inner_im = dot(grouped[p], right_side[target, slot, 1])
-                outer_re = spread[target, slot, 0, p]
-                outer_im = spread[target, slot, 1, p]
-                real = real + fold(outer_re * inner_re - outer_im * inner_im)
-                imag = imag + fold(outer_re * inner_im + outer_im * inner_re)
+            inner_re, inner_im = (
+                jnp.where(
+                    first_slot,
+                    dot(grouped[p], right_side[target, 0, side]),
+                    dot(grouped[p], right_side[target, 1, side]),
+                )
+                for side in range(2)
+            )
+            outer_re = spread[target, 0, p]
+            outer_im = spread[target, 1, p]
+            real = real + fold(outer_re * inner_re - outer_im * inner_im)
+            imag = imag + fold(outer_re * inner_im + outer_im * inner_re)
         return jnp.concatenate([real, imag], axis=0)
 
-    back_left = pltpu.make_async_remote_copy(
-        src_ref=halo_out.at[0], dst_ref=halo_in.at[1], send_sem=halo_send.at[0], recv_sem=halo_recv.at[1],
-        device_id={"rows": lax.rem(row + n_r - 1, n_r)}, device_id_type=MESH,
-    )
-    back_right = pltpu.make_async_remote_copy(
-        src_ref=halo_out.at[1], dst_ref=halo_in.at[0], send_sem=halo_send.at[1], recv_sem=halo_recv.at[0],
-        device_id={"rows": lax.rem(row + 1, n_r)}, device_id_type=MESH,
-    )
+    def give(side):
+        return pltpu.make_async_remote_copy(
+            src_ref=halo_out.at[side],
+            dst_ref=halo_in.at[1 - side],
+            send_sem=halo_send.at[side],
+            recv_sem=halo_recv.at[1 - side],
+            device_id={"rows": lax.rem(row + n_r - 1 + 2 * side, n_r)},
+            device_id_type=MESH,
+        )
 
     @pl.when(jnp.logical_not(has_left))
     def _():
@@ -343,15 +364,14 @@
     def _():
         halo_in[1] = jnp.zeros(halo_in.shape[1:], jnp.float32)
 
-    @pl.when(has_left)
-    def _():
-        halo_out[0] = contribution(0, rows_two)
-        back_left.start()
-
-    @pl.when(has_right)
-    def _():
-        halo_out[1] = contribution(1, rows_two)
-        back_right.start()
+    @pl.loop(0, 2)
+    def _(turn):
+        side = lax.rem(row + turn, 2)
+
+        @pl.when(jnp.logical_or(jnp.logical_and(side == 0, has_left), jnp.logical_and(side == 1, has_right)))
+        def _():
+            halo_out[side] = contribution(side, rows_two)
+            give(side).start()
 
     density = contribution(2, rows_two)
     direct = [jnp.zeros((4, LANES), jnp.float32), jnp.zeros((4, LANES), jnp.float32)]
@@ -362,7 +382,7 @@
             entries = rows_two[p, :, c * LANES : (c + 1) * LANES].astype(jnp.float32)
             direct[c] = direct[c] + fold(jnp.where(on_diagonal, entries, 0.0))
     shape = (LANES, width)
-    place = iota(shape, 1) == iota(shape, 0) + start_v[...]
+    place = iota(shape, 1) == iota(shape, 0) + start[0]
     density = density + dot(
         jnp.concatenate(direct, axis=0).astype(jnp.bfloat16), place.astype(jnp.bfloat16)
     )
@@ -376,39 +396,38 @@
         regroup(land_far, rows_far)
         halo_in[far_side] = contribution(far_side, rows_far)
 
+    @pl.loop(1, n_e)
+    def _(step):
+        exchange(*two, lax.rem(me + step, n_e)).wait_send()
+
+    @pl.when(is_far)
+    def _():
+        @pl.loop(0, n_e)
+        def _(step):
+            cross(step, me).wait_send()
+
+    @pl.when(has_right)
+    def _():
+        to_right.wait_send()
+        give(1).wait_send()
+
     @pl.when(has_left)
     def _():
-        back_right.wait_recv()
+        to_left.wait_send()
+        give(0).wait_send()
+
+    @pl.when(has_left)
+    def _():
+        give(1).wait_recv()
 
     @pl.when(has_right)
     def _():
-        back_left.wait_recv()
+        give(0).wait_recv()
 
     density = density + halo_in[0] + halo_in[1]
     for c in range(2):
         for g in range(2):
             out[g, c] = density[4 * c + 2 * g : 4 * c + 2 * g + 2]
-
-    @pl.loop(1, n_e)
-    def _(step):
-        exchange(*one, step).wait_send()
-        exchange(*two, step).wait_send()
-
-    @pl.when(is_far)
-    def _():
-        @pl.loop(0, n_e)
-        def _(step):
-            cross(step, me).wait_send()
-
-    @pl.when(has_right)
-    def _():
-        to_right.wait_send()
-        back_right.wait_send()
-
-    @pl.when(has_left)
-    def _():
-        to_left.wait_send()
-        back_left.wait_send()
 
 
 def shards(green_window, screened, retarded, energy_order, window_start):
@@ -426,7 +445,6 @@
         pltpu.VMEM((4, total, columns), half),
         pltpu.VMEM((2, 2, slab, width), half),
         pltpu.VMEM((1, total), jnp.int32),
-        pltpu.VMEM((1, 1), jnp.int32),
         pltpu.VMEM((4, total, 4 * total), half),
         pltpu.VMEM((8, entries), full),
         pltpu.VMEM((n_e, 8, per * LANES), half),
@@ -443,7 +461,7 @@
         pltpu.VMEM((2, 2, slab, width), half),
         pltpu.VMEM((2, 2, slab, width), half),
         pltpu.VMEM((3, 2, 2, 2 * LANES, width), half),
-        pltpu.VMEM((3, 2, 2, per, lines, width), full),
+        pltpu.VMEM((3, 2, per, lines, width), full),
         pltpu.VMEM((2, 8, width), full),
         pltpu.VMEM((2, 8, width), full),
         pltpu.SemaphoreType.DMA((7,)),
@@ -462,19 +480,24 @@
     density = pl.pallas_call(
         kernel,
         out_shape=jax.ShapeDtypeStruct((2, 2, 2, width), full),
-        in_specs=[anywhere] * 6,
+        in_specs=[anywhere] * 5 + [pl.BlockSpec(memory_space=pltpu.SMEM)],
         out_specs=pl.BlockSpec(memory_space=pltpu.VMEM),
         scratch_shapes=scratch,
         compiler_params=pltpu.CompilerParams(
-            collective_id=0, has_side_effects=True, vmem_limit_bytes=67043328
+            collective_id=0, has_side_effects=True, vmem_limit_bytes=48 * 2**20
         ),
     )(
-        green_window.reshape(4, 2, entries),
-        screened.reshape(4, total, columns),
-        retarded[:, :, 0],
-        energy_order.reshape(1, total),
-        window_start.reshape(1, 1),
-        jnp.asarray(phase_tables(total)),
+        *[
+            pltpu.with_memory_space_constraint(array, pltpu.HBM)
+            for array in (
+                green_window.reshape(4, 2, entries),
+                screened.reshape(4, total, columns),
+                retarded[:, :, 0],
+                energy_order.reshape(1, total),
+                jnp.asarray(phase_tables(total)),
+            )
+        ],
+        window_start,
     )
     return density[:, :, :, None, :]
 

time: 44.4 us -> 42.6 us (0.959)
  the two profiles are of different devices: /device:TPU:15 before, /device:TPU:7 now
where the time goes in v3:
time: 42.6 us; the launch traced here: 42.5 us
  Pallas kernels  41.2 us (97%)
  between operations  0.66 us (2%)
  local copies, waits for them, and re-layouts  0.61 us (1%)
    pallas_call x1, Pallas kernels, shards(): pl.pallas_call(kernel, out_shape=jax.ShapeDtypeStruct((2, 2, 2, width), f...  41.2 us

profile of v3, /device:TPU:7, one launch (start us, length us, event | category | flops | bytes accessed | tf_op | source)
XLA Modules:
  0.0 42.5 jit_solution(15488234742403276332)
XLA Ops:
  0.7 41.2 %shard_map.64 = f32[2,2,2,192]{3,2,1,0:T(2,128)S(1)} custom-call(bf16[4,2,9216]{2,1,0:T(2,128)(2,1)} %bitcast.8, bf16[4,64,288]{2,1,0:T(8,128)(2,1)} %bitcast.7, bf16[2,2,3,96,192]{4,3,2,1,0:T(8,128)(2,1)} %bitcast.6, s32[1,64]{1,0:T(1,128)} %bitcast.9, bf16[4,64,256]{2,1,0:T(8,128)(2,1)} %constant.2.clone.tables, s32[1]{0:T(128)S(6)} %copy.8.start), custom_call_target="tpu_custom_call" | custom-call | tf_op jit(solution)/shard_map/pallas_call | solution.py:480
  41.9 0.6 %copy.7 = f32[2,2,2,1,192]{4,3,2,1,0:T(1,128)} copy(f32[2,2,2,1,192]{4,2,1,0,3:T(2,128)S(1)} %bitcast.5) | data formatting | bytes 12288 | tf_op jit(solution)/shard_map/broadcast_in_dim | solution.py:502

commit v4 on v3

--- a/solution.py
+++ b/solution.py
@@ -55,11 +55,19 @@
     has_left = jnp.logical_and(row > 0, row != middle)
     has_right = jnp.logical_and(row < n_r - 1, row != middle - 1)
 
+    plane = max(1, n_e // PLANES)
+    planes = n_e // plane
+
+    def far_first(step):
+        turn = step // plane
+        shift = planes // 2 + (turn + 1) // 2 * (1 - 2 * lax.rem(turn, 2))
+        return lax.rem(me // plane + shift, planes) * plane + lax.rem(me + step, plane)
+
     barrier = pltpu.get_barrier_semaphore()
 
     @pl.loop(0, n_e)
     def _(step):
-        other = lax.rem(me + 1 + step, n_e)
+        other = far_first(step)
 
         @pl.when(other != me)
         def _():
@@ -72,6 +80,8 @@
     @pl.when(row < n_r - 1)
     def _():
         pl.semaphore_signal(barrier, inc=1, device_id={"rows": row + 1}, device_id_type=MESH)
+
+    halo_out[...] = jnp.zeros_like(halo_out)
 
     loads = [
         pltpu.make_async_copy(green, green_v, local_sem.at[0]),
@@ -150,7 +160,7 @@
 
     @pl.loop(0, n_e)
     def _(step):
-        other = lax.rem(me + 1 + step, n_e)
+        other = far_first(step)
 
         @pl.when(other != me)
         def _():
@@ -280,8 +290,6 @@
                 c * half : (c + 1) * half, p * LANES : (p + 1) * LANES
             ].reshape(n_e, 4, LANES)
 
-    plane = max(1, n_e // PLANES)
-
     @pl.loop(0, n_e)
     def _(step):
         other = step // plane * plane + lax.rem(me + step, plane)
@@ -370,7 +378,7 @@
 
         @pl.when(jnp.logical_or(jnp.logical_and(side == 0, has_left), jnp.logical_and(side == 1, has_right)))
         def _():
-            halo_out[side] = contribution(side, rows_two)
+            halo_out[side, :, :width] = contribution(side, rows_two)
             give(side).start()
 
     density = contribution(2, rows_two)
@@ -394,7 +402,7 @@
             cross(step, step).wait_recv()
 
         regroup(land_far, rows_far)
-        halo_in[far_side] = contribution(far_side, rows_far)
+        halo_in[far_side, :, :width] = contribution(far_side, rows_far)
 
     @pl.loop(1, n_e)
     def _(step):
@@ -424,7 +432,7 @@
     def _():
         give(0).wait_recv()
 
-    density = density + halo_in[0] + halo_in[1]
+    density = density + halo_in[0, :, :width] + halo_in[1, :, :width]
     for c in range(2):
         for g in range(2):
             out[g, c] = density[4 * c + 2 * g : 4 * c + 2 * g + 2]
@@ -440,6 +448,7 @@
     half = jnp.bfloat16
     full = jnp.float32
     lines = 4 * n_e
+    padded = pl.cdiv(width, LANES) * LANES
     scratch = [
         pltpu.VMEM((4, 2, entries), half),
         pltpu.VMEM((4, total, columns), half),
@@ -462,8 +471,8 @@
         pltpu.VMEM((2, 2, slab, width), half),
         pltpu.VMEM((3, 2, 2, 2 * LANES, width), half),
         pltpu.VMEM((3, 2, per, lines, width), full),
-        pltpu.VMEM((2, 8, width), full),
-        pltpu.VMEM((2, 8, width), full),
+        pltpu.VMEM((2, 8, padded), full),
+        pltpu.VMEM((2, 8, padded), full),
         pltpu.SemaphoreType.DMA((7,)),
         pltpu.SemaphoreType.DMA((n_e,)),
         pltpu.SemaphoreType.DMA((n_e,)),

time: 42.6 us -> 42.1 us (0.988)
  the two profiles are of different devices: /device:TPU:7 before, /device:TPU:15 now
where the time goes in v4:
time: 42.1 us; the launch traced here: 41.5 us
  Pallas kernels  40.2 us (95%)
  between operations  0.66 us (2%)
  local copies, waits for them, and re-layouts  0.61 us (1%)
    pallas_call x1, Pallas kernels, shards(): pl.pallas_call(kernel, out_shape=jax.ShapeDtypeStruct((2, 2, 2, width), f...  40.2 us

profile of v4, /device:TPU:15, one launch (start us, length us, event | category | flops | bytes accessed | tf_op | source)
XLA Modules:
  0.0 41.5 jit_solution(1944072774743762853)
XLA Ops:
  0.7 40.2 %shard_map.64 = f32[2,2,2,192]{3,2,1,0:T(2,128)S(1)} custom-call(bf16[4,2,9216]{2,1,0:T(2,128)(2,1)} %bitcast.8, bf16[4,64,288]{2,1,0:T(8,128)(2,1)} %bitcast.7, bf16[2,2,3,96,192]{4,3,2,1,0:T(8,128)(2,1)} %bitcast.6, s32[1,64]{1,0:T(1,128)} %bitcast.9, bf16[4,64,256]{2,1,0:T(8,128)(2,1)} %constant.2.clone.tables, s32[1]{0:T(128)S(6)} %copy.8.start), custom_call_target="tpu_custom_call" | custom-call | tf_op jit(solution)/shard_map/pallas_call | solution.py:489
  40.9 0.6 %copy.7 = f32[2,2,2,1,192]{4,3,2,1,0:T(1,128)} copy(f32[2,2,2,1,192]{4,2,1,0,3:T(2,128)S(1)} %bitcast.5) | data formatting | bytes 12288 | tf_op jit(solution)/shard_map/broadcast_in_dim | solution.py:511

commit v5 on v4

--- a/solution.py
+++ b/solution.py
@@ -60,7 +60,7 @@
 
     def far_first(step):
         turn = step // plane
-        shift = planes // 2 + (turn + 1) // 2 * (1 - 2 * lax.rem(turn, 2))
+        shift = planes // 2 + (turn + 1) // 2 * (1 - 2 * lax.rem(turn + row, 2))
         return lax.rem(me // plane + shift, planes) * plane + lax.rem(me + step, plane)
 
     barrier = pltpu.get_barrier_semaphore()

time: 42.1 us -> 41.9 us (level)
  no operation moved by 1% of the time
where the time goes in v5:
time: 41.9 us; the launch traced here: 41.5 us
  Pallas kernels  40.2 us (96%)
  between operations  0.66 us (2%)
  local copies, waits for them, and re-layouts  0.61 us (1%)
    pallas_call x1, Pallas kernels, shards(): pl.pallas_call(kernel, out_shape=jax.ShapeDtypeStruct((2, 2, 2, width), f...  40.2 us

profile of v5, /device:TPU:15, one launch (start us, length us, event | category | flops | bytes accessed | tf_op | source)
XLA Modules:
  0.0 41.5 jit_solution(12777601292350795291)
XLA Ops:
  0.7 40.2 %shard_map.64 = f32[2,2,2,192]{3,2,1,0:T(2,128)S(1)} custom-call(bf16[4,2,9216]{2,1,0:T(2,128)(2,1)} %bitcast.8, bf16[4,64,288]{2,1,0:T(8,128)(2,1)} %bitcast.7, bf16[2,2,3,96,192]{4,3,2,1,0:T(8,128)(2,1)} %bitcast.6, s32[1,64]{1,0:T(1,128)} %bitcast.9, bf16[4,64,256]{2,1,0:T(8,128)(2,1)} %constant.2.clone.tables, s32[1]{0:T(128)S(6)} %copy.8.start), custom_call_target="tpu_custom_call" | custom-call | tf_op jit(solution)/shard_map/pallas_call | solution.py:489
  40.9 0.6 %copy.7 = f32[2,2,2,1,192]{4,3,2,1,0:T(1,128)} copy(f32[2,2,2,1,192]{4,2,1,0,3:T(2,128)S(1)} %bitcast.5) | data formatting | bytes 12288 | tf_op jit(solution)/shard_map/broadcast_in_dim | solution.py:511

commit v6 on v5

--- a/solution.py
+++ b/solution.py
@@ -57,6 +57,10 @@
 
     plane = max(1, n_e // PLANES)
     planes = n_e // plane
+
+    def turned(step):
+        turn = step // plane
+        return turn + lax.rem(row, 2) * (1 - 2 * lax.rem(turn, 2))
 
     def far_first(step):
         turn = step // plane
@@ -292,7 +296,7 @@
 
     @pl.loop(0, n_e)
     def _(step):
-        other = step // plane * plane + lax.rem(me + step, plane)
+        other = turned(step) * plane + lax.rem(me + step, plane)
 
         @pl.when(other != me)
         def _():
@@ -302,7 +306,7 @@
     def _():
         @pl.loop(0, n_e)
         def _(step):
-            cross(step // plane * plane + lax.rem(me + step, plane), me).start()
+            cross(turned(step) * plane + lax.rem(me + step, plane), me).start()
 
     land_two[me] = chunks_two[me]
 

time: 41.9 us -> 42 us (level)
  no operation moved by 1% of the time
where the time goes in v6:
time: 42 us; the launch traced here: 41.7 us
  Pallas kernels  40.4 us (96%)
  between operations  0.66 us (2%)
  local copies, waits for them, and re-layouts  0.61 us (1%)
    pallas_call x1, Pallas kernels, shards(): pl.pallas_call(kernel, out_shape=jax.ShapeDtypeStruct((2, 2, 2, width), f...  40.4 us

profile of v6, /device:TPU:15, one launch (start us, length us, event | category | flops | bytes accessed | tf_op | source)
XLA Modules:
  0.0 41.7 jit_solution(10280008872436975400)
XLA Ops:
  0.7 40.4 %shard_map.64 = f32[2,2,2,192]{3,2,1,0:T(2,128)S(1)} custom-call(bf16[4,2,9216]{2,1,0:T(2,128)(2,1)} %bitcast.8, bf16[4,64,288]{2,1,0:T(8,128)(2,1)} %bitcast.7, bf16[2,2,3,96,192]{4,3,2,1,0:T(8,128)(2,1)} %bitcast.6, s32[1,64]{1,0:T(1,128)} %bitcast.9, bf16[4,64,256]{2,1,0:T(8,128)(2,1)} %constant.2.clone.tables, s32[1]{0:T(128)S(6)} %copy.8.start), custom_call_target="tpu_custom_call" | custom-call | tf_op jit(solution)/shard_map/pallas_call | solution.py:493
  41.1 0.6 %copy.7 = f32[2,2,2,1,192]{4,3,2,1,0:T(1,128)} copy(f32[2,2,2,1,192]{4,2,1,0,3:T(2,128)S(1)} %bitcast.5) | data formatting | bytes 12288 | tf_op jit(solution)/shard_map/broadcast_in_dim | solution.py:515
